TPU v7x, 128 devices: a whole 4x4x4 slice. The times are simulated.
128 devices in a mesh: row: 8 (over x, core), col: 16 (over z, y).
Axes of the slice: x: 4, y: 4, z: 4, core: 2. Of those that a mesh axis runs over, the one named last changes fastest.
Arguments:
- raw_vectors: float32 [4096, 81920], P('col', 'row'), may hold values from -810 to 810
- interval_count: int32 [16], replicated, may hold values from 1 to 256, 2048 in all
- cluster_of: int32 [16, 256], P('col'), may hold values from 0 to 31, never falling along the last dimension, each value on 1 to 32 neighbouring positions
- panel_one: float32 [81920, 256], P(('row', 'col')), may hold values from -0.03125 to 0.03125
- factor_one: float32 [256, 256], replicated, may hold values from -0.3 to 2
- panel_two: float32 [81920, 256], P(('row', 'col')), may hold values from -0.03125 to 0.03125
- factor_two: float32 [256, 256], replicated, may hold values from -0.3 to 2
Outputs:
- eigenvectors: float32 [2048, 81920], P('col', 'row')
Inputs may be any that keep to these rules, and one draw needn't show every extreme that they name: `interval_count`: the counts sum to 2048; one is exactly 256. `cluster_of`: labels never fall along an interval's slots; one label covers at most 32 slots, and one covers exactly 32.
All inputs are finite; a program needn't handle non-finite values.
Results may differ from a plain program's by a relative error of at most 0.0003.
Values sent between devices are 32-bit elements; how exact they have to be, the bound alone decides.
A program may use at most 128 MiB of HBM per device.

v0:
```python
import math
import jax
import jax.numpy as jnp
from jax import lax
from jax.sharding import PartitionSpec as P

N = 81920
NB = 16
KD = 128
highest = lax.Precision.HIGHEST


def block_order(counts, column_count, per_device, capacity):
    positions = jnp.arange(column_count * per_device, dtype=jnp.int32)
    device_of = positions // per_device
    local_index = positions % per_device
    rank_of = (local_index // NB * column_count + device_of) * NB + local_index % NB
    interval_end = jnp.cumsum(counts)
    interval_start = interval_end - counts
    owner_device = jnp.sum((interval_end[None, :] <= rank_of[:, None]).astype(jnp.int32), axis=1)
    owner_hit = jnp.arange(column_count, dtype=jnp.int32)[None, :] == owner_device[:, None]
    owner_start = jnp.sum(jnp.where(owner_hit, interval_start[None, :], 0), axis=1)
    return owner_device * capacity + rank_of - owner_start


def finish_block(gram_full, raw_block, labels, is_alive):
    same_group = (labels[:, None] == labels[None, :]) & is_alive[:, None] & is_alive[None, :]
    alive_float = is_alive.astype(jnp.float32)
    masked = jnp.where(same_group, gram_full, 0.0) + jnp.diag(1.0 - alive_float)
    lower_factor = jnp.linalg.cholesky(masked)
    solved = jax.scipy.linalg.solve_triangular(lower_factor, raw_block, lower=True)
    return solved * math.sqrt(N)


def apply_panel(vectors, projected, reflectors, factor):
    scaled = jnp.dot(projected, factor.T, precision=highest, preferred_element_type=jnp.float32)
    return vectors - jnp.einsum("kr,nr->kn", scaled, reflectors, precision=highest)


def project_sum(partial_terms):
    return lax.psum(partial_terms, "row")


def transform(vectors, reflect_one, factor_one, reflect_two, factor_two):
    for reflectors, factor in ((reflect_two, factor_two), (reflect_one, factor_one)):
        partial_terms = jnp.dot(
            vectors, reflectors, precision=highest, preferred_element_type=jnp.float32
        )
        projected = project_sum(partial_terms)
        vectors = apply_panel(vectors, projected, reflectors, factor)
    return vectors


def regroup(vectors):
    return lax.all_to_all(vectors, "col", split_axis=0, concat_axis=1, tiled=True)


def sectioned_order(orthogonal, interval_count, column_count, capacity):
    spread = lax.all_to_all(orthogonal, "col", split_axis=1, concat_axis=0, tiled=True)
    wanted = block_order(interval_count, column_count, KD, capacity)
    return jnp.take(spread, wanted, axis=0)


def body(raw_vectors, interval_count, cluster_of, panel_one, factor_one, panel_two, factor_two):
    column_count = lax.axis_size("col")
    column_index = lax.axis_index("col")
    capacity = raw_vectors.shape[0]
    own_hit = jnp.arange(column_count, dtype=jnp.int32) == column_index
    own_count = jnp.sum(jnp.where(own_hit, interval_count, 0))
    is_alive = jnp.arange(capacity, dtype=jnp.int32) < own_count
    gram_part = jnp.dot(
        raw_vectors, raw_vectors.T, precision=highest, preferred_element_type=jnp.float32
    )
    gram_full = lax.psum(gram_part, "row")
    orthogonal = finish_block(gram_full, raw_vectors, cluster_of[0], is_alive)
    local_rows = regroup(sectioned_order(orthogonal, interval_count, column_count, capacity))
    full_one, full_two = (
        lax.all_gather(panel_one, "col", axis=0, tiled=True),
        lax.all_gather(panel_two, "col", axis=0, tiled=True),
    )
    return transform(local_rows, full_one, factor_one, full_two, factor_two)


def solution(mesh):
    placed = (
        P("col", "row"),
        P(),
        P("col", None),
        P(("row", "col"), None),
        P(),
        P(("row", "col"), None),
        P(),
    )
    return jax.shard_map(
        body, mesh=mesh, in_specs=placed, out_specs=P("col", "row"), check_vma=False
    )
```

profile of v0, /device:TPU:0, one launch (start us, length us, event | category | flops | bytes accessed | tf_op | source)
XLA Modules:
  0.0 624.0 jit_solution(3389111985791579401)
XLA Ops:
  7.4 12.7 %fusion.50 = f32[256,256]{0,1:T(8,128)} fusion(f32[256,10240]{1,0:T(8,128)} %param.7), kind=kOutput, calls=%fused_computation.117 | convolution fusion | flops 8053063680 | bytes 10747904 | tf_op jit(solution)/shard_map/dot_general | solution.py:71
  23.1 61.2 %all-reduce.5.cloned.1.call-done = f32[256,256]{0,1:T(8,128)} async-done(((f32[256,256]{0,1:T(8,128)}), f32[256,256]{0,1:T(8,128)}) %all-reduce.5.cloned.1.call-update) | async-done | bytes 262160 | tf_op jit(solution)/shard_map/psum | solution.py:74
  85.5 1.1 fusion.3
  86.6 11.7 %cholesky.49 = f32[128,128]{1,0:T(8,128)S(1)} custom-call(f32[128,128]{1,0:T(8,128)S(1)} %cholesky.115), custom_call_target="Cholesky" | custom-call | tf_op jit(solution)/shard_map/jit(cholesky)/cholesky | solution.py:30
  98.4 9.8 %custom-call.15 = f32[1,128,128]{1,2,0:T(8,128)S(1)} custom-call(f32[1,128,128]{2,1,0:T(8,128)S(1)} %get-tuple-element.40), custom_call_target="InvertDiagBlocksLowerTriangular" | custom-call | tf_op jit(solution)/shard_map/jit(cholesky)/cholesky | solution.py:30
  108.8 11.7 %cholesky.103 = f32[128,128]{1,0:T(8,128)S(1)} custom-call(f32[128,128]{1,0:T(8,128)S(1)} %convolution_subtract_fusion.3), custom_call_target="Cholesky" | custom-call | tf_op jit(solution)/shard_map/jit(cholesky)/cholesky | solution.py:30
  122.9 4.4 while.1
  123.7 1.4 dynamic-slice.7
  125.8 1.4 dynamic-slice.7
  127.3 19.7 %custom-call.16 = f32[2,128,128]{1,2,0:T(8,128)S(1)} custom-call(f32[2,128,128]{2,1,0:T(8,128)S(1)} %get-tuple-element.12), custom_call_target="InvertDiagBlocksLowerTriangular" | custom-call | tf_op jit(solution)/shard_map/jit(_solve_triangular)/triangular_solve | solution.py:31
  147.0 6.8 %fusion.1 = f32[128,10240]{1,0:T(8,128)S(1)} fusion(f32[256,10240]{1,0:T(8,128)} %param.7, f32[2,128,128]{1,2,0:T(8,128)S(1)} %custom-call.16), kind=kOutput, calls=%fused_computation.9 | convolution fusion | flops 2013265920 | bytes 10551296 | tf_op jit(solution)/shard_map/jit(_solve_triangular)/triangular_solve | solution.py:31
  153.8 2.2 copy-done.2
  156.1 6.4 %fusion = f32[10240,128]{0,1:T(8,128)} fusion(f32[128,10240]{1,0:T(8,128)S(1)} %fusion.1, f32[256,10240]{1,0:T(8,128)S(1)} %copy-done.1, f32[256,256]{0,1:T(8,128)S(1)} %get-tuple-element.98), kind=kOutput, calls=%fused_computation.6 | convolution fusion | flops 2014576640 | bytes 15794176 | tf_op jit(solution)/shard_map/jit(_solve_triangular)/triangular_solve | solution.py:31
  162.5 5.9 copy.56
  168.4 5.5 copy.61
  173.9 6.3 %fusion.5 = f32[128,16,640]{2,0,1:T(8,128)} fusion(f32[16,640,128]{2,1,0:T(8,128)S(1)} %bitcast.76, f32[2,128,128]{1,2,0:T(8,128)S(1)} %custom-call.16), kind=kOutput, calls=%fused_computation.24 | convolution fusion | flops 2013265920 | bytes 10551296 | tf_op jit(solution)/shard_map/jit(_solve_triangular)/triangular_solve | solution.py:31
  180.1 9.0 %maximum_multiply_fusion = f32[256,16,640]{2,0,1:T(8,128)} fusion(f32[128,16,640]{2,0,1:T(8,128)} %fusion.5, f32[128,16,640]{2,0,1:T(8,128)} %bitcast.75), kind=kLoop, calls=%fused_computation.7 | loop fusion | flops 5242880 | bytes 20971520 | tf_op jit(solution)/shard_map/mul | solution.py:32
  189.1 6.8 %all-to-all-start = ((f32[256,16,640]{2,0,1:T(8,128)}), f32[256,16,640]{2,0,1:T(8,128)}, u32[]{:S(2)}, u32[]{:S(2)}) async-start(f32[256,16,640]{2,0,1:T(8,128)} %maximum_multiply_fusion), calls=%async_computation | async-start | bytes 20971520 | tf_op jit(solution)/shard_map/all_to_all | solution.py:59
  196.3 149.8 %all-to-all-done = f32[256,16,640]{2,0,1:T(8,128)} async-done(((f32[256,16,640]{2,0,1:T(8,128)}), f32[256,16,640]{2,0,1:T(8,128)}, u32[]{:S(2)}, u32[]{:S(2)}) %all-to-all-start) | async-done | bytes 10485792 | tf_op jit(solution)/shard_map/all_to_all | solution.py:59
  346.1 14.1 %gather_fusion = f32[2048,640]{1,0:T(8,128)} fusion(f32[4096,640]{1,0:T(8,128)} %bitcast.13, s32[2048]{0:T(1024)S(1)} %broadcast_clamp_fusion), kind=kCustom, calls=%fused_computation | custom fusion | bytes 10493952 | tf_op jit(solution)/shard_map/jit(_take)/gather | solution.py:61
  360.2 2.8 broadcast_select_fusion
  363.0 63.6 %all_to_all.32 = f32[16,128,640]{2,1,0:T(8,128)S(1)} all-to-all(f32[16,128,640]{2,1,0:T(8,128)S(1)} %broadcast_select_fusion), channel_id=1, replica_groups=mesh['row'=8,'col'=16] {'col'}, dimensions={0} | all-to-all | bytes 10485760 | tf_op jit(solution)/shard_map/all_to_all | solution.py:55
  426.5 2.9 copy.59
  429.4 9.2 %fusion.51 = f32[128,256]{1,0:T(8,128)} fusion(f32[128,10240]{1,0:T(8,128)} %bitcast.72, f32[10240,256]{1,0:T(8,128)} %all-gather.3.cloned.1.call-done), kind=kOutput, calls=%fused_computation.118 | convolution fusion | flops 4026531840 | bytes 15859712 | tf_op jit(solution)/shard_map/dot_general | solution.py:46
  439.3 66.5 %all-reduce.7.cloned.1.call-done = f32[128,256]{1,0:T(8,128)} async-done(((f32[128,256]{1,0:T(8,128)}), f32[128,256]{1,0:T(8,128)}) %all-reduce.7.cloned.1.call-update) | async-done | bytes 131088 | tf_op jit(solution)/shard_map/psum | solution.py:41
  505.8 1.3 fusion.52
  507.1 18.8 %convolution_subtract_fusion.1 = f32[128,10240]{1,0:T(8,128)} fusion(f32[128,10240]{1,0:T(8,128)} %bitcast.73, f32[128,256]{1,0:T(8,128)S(1)} %fusion.52, f32[10240,256]{1,0:T(8,128)} %all-gather.3.cloned.1.call-done), kind=kOutput, calls=%fused_computation.4 | convolution fusion | flops 4027842560 | bytes 21102592 | tf_op jit(solution)/shard_map/kr,nr->kn/dot_general | solution.py:37
  525.9 1.7 all-gather.5.cloned.1.call-done
  527.6 9.5 %fusion.53 = f32[128,256]{1,0:T(8,128)} fusion(f32[128,10240]{1,0:T(8,128)} %convolution_subtract_fusion.1, f32[10240,256]{1,0:T(8,128)} %all-gather.5.cloned.1.call-done), kind=kOutput, calls=%fused_computation.120 | convolution fusion | flops 4026531840 | bytes 15859712 | tf_op jit(solution)/shard_map/dot_general | solution.py:46
  537.1 59.6 %all-reduce.9.cloned.1.call-done = f32[128,256]{1,0:T(8,128)} async-done(((f32[128,256]{1,0:T(8,128)}), f32[128,256]{1,0:T(8,128)}) %all-reduce.9.cloned.1.call-update) | async-done | bytes 131088 | tf_op jit(solution)/shard_map/psum | solution.py:41
  596.7 1.3 fusion.54
  598.0 18.4 %convolution_subtract_fusion = f32[128,10240]{1,0:T(8,128)} fusion(f32[128,10240]{1,0:T(8,128)} %convolution_subtract_fusion.1, f32[128,256]{1,0:T(8,128)S(1)} %fusion.54, f32[10240,256]{1,0:T(8,128)} %all-gather.5.cloned.1.call-done), kind=kOutput, calls=%fused_computation.3 | convolution fusion | flops 4027842560 | bytes 21102592 | tf_op jit(solution)/shard_map/kr,nr->kn/dot_general | solution.py:37
  (63 shorter events, 8.2 us)
Async XLA Ops:
  7.4 498.4 %copy-start = (f32[256,256]{1,0:T(8,128)S(1)}, f32[256,256]{1,0:T(8,128)}, u32[]{:S(2)}) copy-start(f32[256,256]{1,0:T(8,128)} %param.13) | copy-start | bytes 786436
  7.4 13.3 %copy-start.6 = (s32[16]{0:T(128)S(1)}, s32[16]{0:T(128)}, u32[]{:S(2)}) copy-start(s32[16]{0:T(128)} %param.8) | copy-start | bytes 196
  7.4 76.9 %copy-start.5 = (s32[1,256]{1,0:T(1,128)S(1)}, s32[1,256]{1,0:T(1,128)}, u32[]{:S(2)}) copy-start(s32[1,256]{1,0:T(1,128)} %param.9) | copy-start | bytes 3076
  7.4 76.9 %all-reduce.5.cloned.1.call-start = ((), (), s32[]{:S(2)}) async-start(), calls=%async_computation.2 | async-start | bytes 524288 | tf_op jit(solution)/shard_map/psum | solution.py:74
  20.1 409.3 %all-gather.3.cloned.1.call-start = ((), (), s32[]{:S(2)}) async-start(), calls=%async_computation.3 | async-start | bytes 11141120 | tf_op jit(solution)/shard_map/all_gather | solution.py:79
  147.0 9.1 %copy-start.1 = (f32[256,10240]{1,0:T(8,128)S(1)}, f32[256,10240]{1,0:T(8,128)}, u32[]{:S(2)}) copy-start(f32[256,10240]{1,0:T(8,128)} %param.7) | copy-start | bytes 31457284
  153.8 2.2 copy-start.2
  168.4 5.5 copy-start.3
  189.1 157.0 %all-to-all-start = ((f32[256,16,640]{2,0,1:T(8,128)}), f32[256,16,640]{2,0,1:T(8,128)}, u32[]{:S(2)}, u32[]{:S(2)}) async-start(f32[256,16,640]{2,0,1:T(8,128)} %maximum_multiply_fusion), calls=%async_computation | async-start | bytes 20971520 | tf_op jit(solution)/shard_map/all_to_all | solution.py:59
  195.9 309.9 %all-reduce.7.cloned.1.call-start = ((), (), s32[]{:S(2)}) async-start(), calls=%async_computation.4 | async-start | bytes 262144 | tf_op jit(solution)/shard_map/psum | solution.py:41
  438.7 89.0 %all-gather.5.cloned.1.call-start = ((), (), s32[]{:S(2)}) async-start(), calls=%async_computation.5 | async-start | bytes 11141120 | tf_op jit(solution)/shard_map/all_gather | solution.py:78
  439.3 157.4 %all-reduce.9.cloned.1.call-start = ((), (), s32[]{:S(2)}) async-start(), calls=%async_computation.6 | async-start | bytes 262144 | tf_op jit(solution)/shard_map/psum | solution.py:41
  525.9 70.8 %copy-start.4 = (f32[256,256]{1,0:T(8,128)S(1)}, f32[256,256]{1,0:T(8,128)}, u32[]{:S(2)}) copy-start(f32[256,256]{1,0:T(8,128)} %param.11) | copy-start | bytes 786436
Sparse Core Ops, SparseCore 0:
  20.2 63.9 all-reduce.4
  438.8 66.9 all-reduce.6
  537.3 59.3 all-reduce.8
Sparse Core Ops, SparseCore 1:
  22.7 83.0 all-gather.2
  441.3 86.3 all-gather.4
where the time goes:
time: 627 us; the launch traced here: 624 us
  waiting for transfers between devices  339 us (54%)
  matrix products  91.2 us (15%)
  other arithmetic  70.2 us (11%)
  blocking collectives  63.6 us (10%)
  local copies, waits for them, and re-layouts  35.4 us (6%)
  between operations  16.6 us (3%)
  starting transfers between devices  7.52 us (1%)
    all_to_all x1, waiting for transfers between devices, sectioned_order(): lax.all_to_all(orthogonal, 'col', split_axis=1, concat_axis=0, tiled=True)  150 us
    psum x2, waiting for transfers between devices, project_sum(): return lax.psum(partial_terms, 'row')  126 us
    all_to_all x1, blocking collectives, regroup(): lax.all_to_all(vectors, 'col', split_axis=0, concat_axis=1, tiled=True)  63.6 us
    psum x1, waiting for transfers between devices, body(): gram_full = lax.psum(gram_part, 'row')  61.2 us
    dot_general x2, matrix products, apply_panel(): jnp.einsum('kr,nr->kn', scaled, reflectors, precision=highest)  37.3 us
    another operation x6, other arithmetic, finish_block(): lower_factor = jnp.linalg.cholesky(masked)  34 us
    another operation x3, other arithmetic, finish_block(): jax.scipy.linalg.solve_triangular(lower_factor, raw_block, lower=True)  19.7 us
    another operation x3, matrix products, finish_block(): jax.scipy.linalg.solve_triangular(lower_factor, raw_block, lower=True)  19.5 us
  transfers between devices with their start and end apart: 6, of which 5 were waited for; matrix products, arithmetic and copies ran while one was open for 23% of the time, Pallas kernels for 0%

commit v1 on v0

--- a/solution.py
+++ b/solution.py
@@ -8,6 +8,10 @@
 NB = 16
 KD = 128
 highest = lax.Precision.HIGHEST
+
+
+def close_frame(mine_x):
+    return lax.all_gather(mine_x, axis_name="row").sum(axis=0)
 
 
 def block_order(counts, column_count, per_device, capacity):
@@ -71,7 +75,7 @@
     gram_part = jnp.dot(
         raw_vectors, raw_vectors.T, precision=highest, preferred_element_type=jnp.float32
     )
-    gram_full = lax.psum(gram_part, "row")
+    gram_full = close_frame(gram_part)
     orthogonal = finish_block(gram_full, raw_vectors, cluster_of[0], is_alive)
     local_rows = regroup(sectioned_order(orthogonal, interval_count, column_count, capacity))
     full_one, full_two = (

time: 627 us -> 649 us (1.035)
  waiting for transfers between devices: 339 us -> 360 us
    psum x1 -> x0, waiting for transfers between devices: 61.2 us -> none  [body(): gram_full = lax.psum(gram_part, 'row')]
    all_gather x1, waiting for transfers between devices: 1.72 us -> 61.7 us  [body(): lax.all_gather(panel_one, 'col', axis=0, tiled=True)]
    all_gather x0 -> x1, waiting for transfers between devices: none -> 24.8 us  [close_frame(): return lax.all_gather(mine_x, axis_name='row').sum(axis=0)]
    psum x2, waiting for transfers between devices: 126 us -> 115 us  [project_sum(): return lax.psum(partial_terms, 'row')]
    all_to_all x1, waiting for transfers between devices: 150 us -> 157 us  [sectioned_order(): lax.all_to_all(orthogonal, 'col', split_axis=1, concat_axis=0, tiled=True)]
  transfers between devices with their start and end apart: 6 -> 6, of which waited for: 5 -> 5; matrix products, arithmetic and copies ran while one was open for 23% -> 22% of each run, Pallas kernels for 0% -> 0%
where the time goes in v1:
time: 649 us; the launch traced here: 644 us
  waiting for transfers between devices  360 us (55%)
  matrix products  91.6 us (14%)
  other arithmetic  70 us (11%)
  blocking collectives  65.5 us (10%)
  local copies, waits for them, and re-layouts  35.1 us (5%)
  between operations  14.9 us (2%)
  starting transfers between devices  7.31 us (1%)
    all_to_all x1, waiting for transfers between devices, sectioned_order(): lax.all_to_all(orthogonal, 'col', split_axis=1, concat_axis=0, tiled=True)  157 us
    psum x2, waiting for transfers between devices, project_sum(): return lax.psum(partial_terms, 'row')  115 us
    all_to_all x1, blocking collectives, regroup(): lax.all_to_all(vectors, 'col', split_axis=0, concat_axis=1, tiled=True)  65.5 us
    all_gather x1, waiting for transfers between devices, body(): lax.all_gather(panel_one, 'col', axis=0, tiled=True)  61.7 us
    dot_general x2, matrix products, apply_panel(): jnp.einsum('kr,nr->kn', scaled, reflectors, precision=highest)  36.9 us
    another operation x6, other arithmetic, finish_block(): lower_factor = jnp.linalg.cholesky(masked)  34 us
    all_gather x1, waiting for transfers between devices, close_frame(): return lax.all_gather(mine_x, axis_name='row').sum(axis=0)  24.8 us
    another operation x3, other arithmetic, finish_block(): jax.scipy.linalg.solve_triangular(lower_factor, raw_block, lower=True)  19.7 us
  transfers between devices with their start and end apart: 6, of which 5 were waited for; matrix products, arithmetic and copies ran while one was open for 22% of the time, Pallas kernels for 0%

profile of v1, /device:TPU:0, one launch (start us, length us, event | category | flops | bytes accessed | tf_op | source)
XLA Modules:
  0.0 644.1 jit_solution(2422682928386055619)
XLA Ops:
  6.5 13.6 %fusion.52 = f32[256,256]{1,0:T(8,128)} fusion(f32[256,10240]{1,0:T(8,128)} %param.7), kind=kOutput, calls=%fused_computation.119 | convolution fusion | flops 8053063680 | bytes 10747904 | tf_op jit(solution)/shard_map/dot_general | solution.py:75
  23.2 24.8 %all-gather.9.cloned.1.call-done = f32[2048,256]{1,0:T(8,128)} async-done(((f32[256,256]{1,0:T(8,128)}), f32[2048,256]{1,0:T(8,128)}) %all-gather.9.cloned.1.call-update) | async-done | bytes 2097168 | tf_op jit(solution)/shard_map/all_gather | solution.py:14
  48.1 1.8 reduce_sum.46
  50.2 11.7 %cholesky.49 = f32[128,128]{1,0:T(8,128)S(1)} custom-call(f32[128,128]{1,0:T(8,128)S(1)} %cholesky.115), custom_call_target="Cholesky" | custom-call | tf_op jit(solution)/shard_map/jit(cholesky)/cholesky | solution.py:34
  62.0 9.8 %custom-call.15 = f32[1,128,128]{1,2,0:T(8,128)S(1)} custom-call(f32[1,128,128]{2,1,0:T(8,128)S(1)} %get-tuple-element.26), custom_call_target="InvertDiagBlocksLowerTriangular" | custom-call | tf_op jit(solution)/shard_map/jit(cholesky)/cholesky | solution.py:34
  72.3 11.7 %cholesky.103 = f32[128,128]{1,0:T(8,128)S(1)} custom-call(f32[128,128]{1,0:T(8,128)S(1)} %convolution_subtract_fusion.3), custom_call_target="Cholesky" | custom-call | tf_op jit(solution)/shard_map/jit(cholesky)/cholesky | solution.py:34
  86.2 4.2 while.1
  87.0 1.4 bitcast_dynamic-update-slice_fusion.2
  89.0 1.4 bitcast_dynamic-update-slice_fusion.2
  90.4 19.7 %custom-call.16 = f32[2,128,128]{1,2,0:T(8,128)S(1)} custom-call(f32[2,128,128]{2,1,0:T(8,128)S(1)} %get-tuple-element.12), custom_call_target="InvertDiagBlocksLowerTriangular" | custom-call | tf_op jit(solution)/shard_map/jit(_solve_triangular)/triangular_solve | solution.py:35
  110.1 6.9 %fusion.1 = f32[128,10240]{1,0:T(8,128)S(1)} fusion(f32[256,10240]{1,0:T(8,128)} %param.7, f32[2,128,128]{1,2,0:T(8,128)S(1)} %custom-call.16), kind=kOutput, calls=%fused_computation.9 | convolution fusion | flops 2013265920 | bytes 10551296 | tf_op jit(solution)/shard_map/jit(_solve_triangular)/triangular_solve | solution.py:35
  117.0 2.2 copy-done.2
  119.2 6.3 fusion
  125.6 5.9 copy.41
  131.4 5.5 copy.45
  136.9 6.3 fusion.7
  143.2 9.0 %maximum_multiply_fusion = f32[256,16,640]{2,0,1:T(8,128)} fusion(f32[128,16,640]{2,0,1:T(8,128)} %fusion.7, f32[128,16,640]{2,0,1:T(8,128)} %bitcast.82), kind=kLoop, calls=%fused_computation.7 | loop fusion | flops 5242880 | bytes 20971520 | tf_op jit(solution)/shard_map/mul | solution.py:36
  152.1 7.0 %all-to-all-start = ((f32[256,16,640]{2,0,1:T(8,128)}), f32[256,16,640]{2,0,1:T(8,128)}, u32[]{:S(2)}, u32[]{:S(2)}) async-start(f32[256,16,640]{2,0,1:T(8,128)} %maximum_multiply_fusion), calls=%async_computation | async-start | bytes 20971520 | tf_op jit(solution)/shard_map/all_to_all | solution.py:63
  159.5 156.8 %all-to-all-done = f32[256,16,640]{2,0,1:T(8,128)} async-done(((f32[256,16,640]{2,0,1:T(8,128)}), f32[256,16,640]{2,0,1:T(8,128)}, u32[]{:S(2)}, u32[]{:S(2)}) %all-to-all-start) | async-done | bytes 10485792 | tf_op jit(solution)/shard_map/all_to_all | solution.py:63
  316.3 14.3 %gather_fusion = f32[2048,640]{1,0:T(8,128)} fusion(f32[4096,640]{1,0:T(8,128)} %bitcast.14, s32[2048]{0:T(1024)S(1)} %broadcast_clamp_fusion), kind=kCustom, calls=%fused_computation | custom fusion | bytes 10493952 | tf_op jit(solution)/shard_map/jit(_take)/gather | solution.py:65
  330.6 2.8 broadcast_select_fusion
  333.4 65.5 %all_to_all.32 = f32[16,128,640]{2,1,0:T(8,128)S(1)} all-to-all(f32[16,128,640]{2,1,0:T(8,128)S(1)} %broadcast_select_fusion), channel_id=1, replica_groups=mesh['row'=8,'col'=16] {'col'}, dimensions={0} | all-to-all | bytes 10485760 | tf_op jit(solution)/shard_map/all_to_all | solution.py:59
  398.9 2.9 copy.43
  401.8 9.2 %fusion.53 = f32[128,256]{1,0:T(8,128)} fusion(f32[128,10240]{1,0:T(8,128)} %bitcast.79, f32[10240,256]{1,0:T(8,128)} %all-gather.5.cloned.1.call-done), kind=kOutput, calls=%fused_computation.120 | convolution fusion | flops 4026531840 | bytes 15859712 | tf_op jit(solution)/shard_map/dot_general | solution.py:50
  411.6 55.6 %all-reduce.4.cloned.1.call-done = f32[128,256]{1,0:T(8,128)} async-done(((f32[128,256]{1,0:T(8,128)}), f32[128,256]{1,0:T(8,128)}) %all-reduce.4.cloned.1.call-update) | async-done | bytes 131088 | tf_op jit(solution)/shard_map/psum | solution.py:45
  467.2 1.3 fusion.54
  468.5 18.4 %convolution_subtract_fusion.1 = f32[128,10240]{1,0:T(8,128)} fusion(f32[128,10240]{1,0:T(8,128)} %bitcast.80, f32[128,256]{1,0:T(8,128)S(1)} %fusion.54, f32[10240,256]{1,0:T(8,128)} %all-gather.5.cloned.1.call-done), kind=kOutput, calls=%fused_computation.4 | convolution fusion | flops 4027842560 | bytes 21102592 | tf_op jit(solution)/shard_map/kr,nr->kn/dot_general | solution.py:41
  486.9 61.7 %all-gather.7.cloned.1.call-done = f32[10240,256]{1,0:T(8,128)} async-done(((f32[640,256]{1,0:T(8,128)}), f32[10240,256]{1,0:T(8,128)}) %all-gather.7.cloned.1.call-update) | async-done | bytes 10485776 | tf_op jit(solution)/shard_map/all_gather | solution.py:82
  548.7 9.4 %fusion.55 = f32[128,256]{1,0:T(8,128)} fusion(f32[128,10240]{1,0:T(8,128)} %convolution_subtract_fusion.1, f32[10240,256]{1,0:T(8,128)} %all-gather.7.cloned.1.call-done), kind=kOutput, calls=%fused_computation.122 | convolution fusion | flops 4026531840 | bytes 15859712 | tf_op jit(solution)/shard_map/dot_general | solution.py:50
  558.1 59.6 %all-reduce.6.cloned.1.call-done = f32[128,256]{1,0:T(8,128)} async-done(((f32[128,256]{1,0:T(8,128)}), f32[128,256]{1,0:T(8,128)}) %all-reduce.6.cloned.1.call-update) | async-done | bytes 131088 | tf_op jit(solution)/shard_map/psum | solution.py:45
  617.7 1.3 fusion.56
  619.0 18.4 %convolution_subtract_fusion = f32[128,10240]{1,0:T(8,128)} fusion(f32[128,10240]{1,0:T(8,128)} %convolution_subtract_fusion.1, f32[128,256]{1,0:T(8,128)S(1)} %fusion.56, f32[10240,256]{1,0:T(8,128)} %all-gather.7.cloned.1.call-done), kind=kOutput, calls=%fused_computation.3 | convolution fusion | flops 4027842560 | bytes 21102592 | tf_op jit(solution)/shard_map/kr,nr->kn/dot_general | solution.py:41
  (54 shorter events, 7.0 us)
Async XLA Ops:
  6.5 460.7 %copy-start = (f32[256,256]{1,0:T(8,128)S(1)}, f32[256,256]{1,0:T(8,128)}, u32[]{:S(2)}) copy-start(f32[256,256]{1,0:T(8,128)} %param.13) | copy-start | bytes 786436
  6.5 14.4 %copy-start.6 = (s32[16]{0:T(128)S(1)}, s32[16]{0:T(128)}, u32[]{:S(2)}) copy-start(s32[16]{0:T(128)} %param.8) | copy-start | bytes 196
  6.5 43.4 %copy-start.5 = (s32[1,256]{1,0:T(1,128)S(1)}, s32[1,256]{1,0:T(1,128)}, u32[]{:S(2)}) copy-start(s32[1,256]{1,0:T(1,128)} %param.9) | copy-start | bytes 3076
  6.5 41.5 %all-gather.9.cloned.1.call-start = ((), (), s32[]{:S(2)}) async-start(), calls=%async_computation.6 | async-start | bytes 2359296 | tf_op jit(solution)/shard_map/all_gather | solution.py:14
  20.1 381.6 %all-gather.5.cloned.1.call-start = ((), (), s32[]{:S(2)}) async-start(), calls=%async_computation.2 | async-start | bytes 11141120 | tf_op jit(solution)/shard_map/all_gather | solution.py:83
  110.1 9.1 %copy-start.1 = (f32[256,10240]{1,0:T(8,128)S(1)}, f32[256,10240]{1,0:T(8,128)}, u32[]{:S(2)}) copy-start(f32[256,10240]{1,0:T(8,128)} %param.7) | copy-start | bytes 31457284
  117.0 2.2 copy-start.2
  131.4 5.5 copy-start.3
  152.1 164.1 %all-to-all-start = ((f32[256,16,640]{2,0,1:T(8,128)}), f32[256,16,640]{2,0,1:T(8,128)}, u32[]{:S(2)}, u32[]{:S(2)}) async-start(f32[256,16,640]{2,0,1:T(8,128)} %maximum_multiply_fusion), calls=%async_computation | async-start | bytes 20971520 | tf_op jit(solution)/shard_map/all_to_all | solution.py:63
  159.1 308.1 %all-reduce.4.cloned.1.call-start = ((), (), s32[]{:S(2)}) async-start(), calls=%async_computation.3 | async-start | bytes 262144 | tf_op jit(solution)/shard_map/psum | solution.py:45
  411.0 137.7 %all-gather.7.cloned.1.call-start = ((), (), s32[]{:S(2)}) async-start(), calls=%async_computation.4 | async-start | bytes 11141120 | tf_op jit(solution)/shard_map/all_gather | solution.py:82
  411.6 206.1 %all-reduce.6.cloned.1.call-start = ((), (), s32[]{:S(2)}) async-start(), calls=%async_computation.5 | async-start | bytes 262144 | tf_op jit(solution)/shard_map/psum | solution.py:45
  486.9 130.7 %copy-start.4 = (f32[256,256]{1,0:T(8,128)S(1)}, f32[256,256]{1,0:T(8,128)}, u32[]{:S(2)}) copy-start(f32[256,256]{1,0:T(8,128)} %param.11) | copy-start | bytes 786436
Sparse Core Ops, SparseCore 0:
  20.3 27.7 all-gather.8
  50.2 81.0 all-gather.4
  411.1 56.0 all-reduce.3
  469.2 79.4 all-gather.6
  558.2 59.4 all-reduce.5
